TPU v7x, 32 devices: a whole 2x2x4 slice. The times are simulated.
32 devices in a mesh: node: 4 (over y, x), feat: 4 (over z), tm: 2 (over core).
Axes of the slice: x: 2, y: 2, z: 4, core: 2. Of those that a mesh axis runs over, the one named last changes fastest.
Arguments:
- tensor: float32 [2, 16384, 4096], P('tm', 'node', 'feat'), may hold values from -6 to 6
- basis: float32 [16384, 128], P('node'), may hold values from -0.046875 to 0.046875
Outputs:
- gram: float32 [4096, 4096], P('feat', ('node', 'tm'))
All inputs are finite; a program needn't handle non-finite values.
Results may differ from a plain program's by a relative error of at most 0.000073.
Values sent between devices are 32-bit elements; how exact they have to be, the bound alone decides.
No kernel may reach another device: no remote copies, remote signals or barrier semaphores. Data moves between devices by JAX's collectives and lax.ppermute only.
A program may use at most 128 MiB of HBM per device.

v0:
```python
import jax
import jax.numpy as jnp
from jax import lax
from jax.sharding import PartitionSpec as P


def body(tensor, basis):
    local_data = tensor[0]
    partial_proj = lax.dot_general(
        basis,
        local_data,
        (((0,), (0,)), ((), ())),
        precision=lax.Precision.HIGHEST,
        preferred_element_type=jnp.float32,
    )
    scale = 1.0 / (basis.shape[1] * lax.axis_size("tm"))
    block_proj = lax.psum(partial_proj, "node")
    full_proj = lax.all_gather(block_proj, "feat", axis=1, tiled=True)
    width = full_proj.shape[1] // lax.axis_size("node")
    columns = lax.dynamic_slice_in_dim(full_proj, lax.axis_index("node") * width, width, 1)
    term = lax.dot_general(
        block_proj,
        columns,
        (((0,), (0,)), ((), ())),
        precision=lax.Precision.HIGHEST,
        preferred_element_type=jnp.float32,
    )
    result = lax.psum_scatter(term * scale, "tm", scatter_dimension=1, tiled=True)
    return result


def solution(mesh):
    in_specs = (P("tm", "node", "feat"), P("node", None))
    out_specs = P("feat", ("node", "tm"))
    return jax.shard_map(body, mesh=mesh, in_specs=in_specs, out_specs=out_specs, check_vma=False)
```

profile of v0, /device:TPU:0, one launch (start us, length us, event | category | flops | bytes accessed | tf_op | source)
XLA Modules:
  0.0 141.4 jit_solution(4735564744402768312)
XLA Ops:
  6.5 0.0 copy-start
  6.5 0.0 all-reduce.2.cloned.1.call-start
  6.5 1.6 %copy-done = f32[4096,128]{1,0:T(8,128)S(1)} copy-done((f32[4096,128]{1,0:T(8,128)S(1)}, f32[4096,128]{1,0:T(8,128)}, u32[]{:S(2)}) %copy-start) | copy-done | bytes 2097176
  8.1 13.5 %fusion = f32[128,1024]{1,0:T(8,128)} fusion(f32[4096,128]{1,0:T(8,128)S(1)} %copy-done, f32[1,4096,1024]{2,1,0:T(8,128)} %param.2), kind=kOutput, calls=%fused_computation | convolution fusion | flops 6442450944 | bytes 19398656 | tf_op jit(solution)/shard_map/dot_general | solution.py:9
  21.6 0.0 all-reduce.2.cloned.1.call-update
  21.6 0.0 all-gather.2.cloned.1.call-start
  21.7 48.1 %all-reduce.2.cloned.1.call-done = f32[128,1024]{1,0:T(8,128)} async-done(((f32[128,1024]{1,0:T(8,128)}), f32[128,1024]{1,0:T(8,128)}) %all-reduce.2.cloned.1.call-update) | async-done | bytes 524304 | tf_op jit(solution)/shard_map/psum | solution.py:17
  69.8 0.0 all-gather.2.cloned.1.call-update
  69.8 0.0 reduce-scatter.2.cloned.1.call-start
  69.9 47.5 %all-gather.2.cloned.1.call-done = f32[128,4096]{1,0:T(8,128)} async-done(((f32[128,1024]{1,0:T(8,128)}), f32[128,4096]{1,0:T(8,128)}) %all-gather.2.cloned.1.call-update) | async-done | bytes 2097168 | tf_op jit(solution)/shard_map/all_gather | solution.py:18
  117.3 6.6 %convolution_multiply_fusion = f32[1024,1024]{1,0:T(8,128)} fusion(f32[128,1024]{1,0:T(8,128)} %all-reduce.2.cloned.1.call-done, f32[128,4096]{1,0:T(8,128)} %all-gather.2.cloned.1.call-done, s32[]{:T(128)S(6)} %select_n.3), kind=kOutput, calls=%fused_computation.2 | convolution fusion | flops 1611661312 | bytes 5242884 | tf_op jit(solution)/shard_map/dot_general | solution.py:21
  124.0 0.0 reduce-scatter.2.cloned.1.call-update
  124.0 10.9 %reduce-scatter.2.cloned.1.call-done = f32[1024,512]{1,0:T(8,128)} async-done(((f32[1024,1024]{1,0:T(8,128)}), f32[1024,512]{1,0:T(8,128)}) %reduce-scatter.2.cloned.1.call-update) | async-done | bytes 2097168 | tf_op jit(solution)/shard_map/reduce_scatter | solution.py:28
Async XLA Ops:
  6.5 1.6 %copy-start = (f32[4096,128]{1,0:T(8,128)S(1)}, f32[4096,128]{1,0:T(8,128)}, u32[]{:S(2)}) copy-start(f32[4096,128]{1,0:T(8,128)} %param.3) | copy-start | bytes 6291460
  6.5 63.3 %all-reduce.2.cloned.1.call-start = ((), (), s32[]{:S(2)}) async-start(), calls=%async_computation.1 | async-start | bytes 1048576 | tf_op jit(solution)/shard_map/psum | solution.py:17
  21.6 95.7 %all-gather.2.cloned.1.call-start = ((), (), s32[]{:S(2)}) async-start(), calls=%async_computation.2 | async-start | bytes 2621440 | tf_op jit(solution)/shard_map/all_gather | solution.py:18
  69.8 65.1 %reduce-scatter.2.cloned.1.call-start = ((), (), s32[]{:S(2)}) async-start(), calls=%async_computation.3 | async-start | bytes 6291456 | tf_op jit(solution)/shard_map/reduce_scatter | solution.py:28
Sparse Core Ops, SparseCore 0:
  21.7 48.0 all-reduce.1
  71.4 45.9 all-gather.1
  124.1 10.7 reduce-scatter.1
where the time goes:
time: 142 us; the launch traced here: 141 us
  waiting for transfers between devices  107 us (75%)
  matrix products  20.1 us (14%)
  between operations  13.1 us (9%)
  local copies, waits for them, and re-layouts  1.59 us (1%)
    psum x1, waiting for transfers between devices, body(): block_proj = lax.psum(partial_proj, 'node')  48.1 us
    all_gather x1, waiting for transfers between devices, body(): full_proj = lax.all_gather(block_proj, 'feat', axis=1, tiled=True)  47.5 us
    dot_general x1, matrix products, body(): lax.dot_general(basis, local_data, (((0,), (0,)), ((), ())), precision=la...  13.5 us
    reduce_scatter x1, waiting for transfers between devices, body(): lax.psum_scatter(term * scale, 'tm', scatter_dimension=1, tiled=True)  10.9 us
    dot_general x1, matrix products, body(): lax.dot_general(block_proj, columns, (((0,), (0,)), ((), ())), precision=...  6.61 us
  transfers between devices with their start and end apart: 3, of which 3 were waited for; matrix products, arithmetic and copies ran while one was open for 0% of the time, Pallas kernels for 0%

commit v1 on v0

--- a/solution.py
+++ b/solution.py
@@ -2,6 +2,27 @@
 import jax.numpy as jnp
 from jax import lax
 from jax.sharding import PartitionSpec as P
+
+
+def ring_gather(value, axis, dim):
+    length, index, rows = (lax.axis_size(axis), lax.axis_index(axis), value.shape[dim])
+    right = [(i, (i + 1) % length) for i in range(length)]
+    left = [(i, (i - 1) % length) for i in range(length)]
+    out = jnp.zeros((*value.shape[:dim], length * rows, *value.shape[dim + 1 :]), value.dtype)
+    out = lax.dynamic_update_slice_in_dim(out, value, index * rows, axis=dim)
+    from_left = from_right = value
+    half = length // 2
+    for turn in range(1, half + 1):
+        from_left = lax.ppermute(from_left, axis, right)
+        out = lax.dynamic_update_slice_in_dim(
+            out, from_left, (index - turn) % length * rows, axis=dim
+        )
+        if turn < length - half:
+            from_right = lax.ppermute(from_right, axis, left)
+            out = lax.dynamic_update_slice_in_dim(
+                out, from_right, (index + turn) % length * rows, axis=dim
+            )
+    return out
 
 
 def body(tensor, basis):
@@ -15,7 +36,7 @@
     )
     scale = 1.0 / (basis.shape[1] * lax.axis_size("tm"))
     block_proj = lax.psum(partial_proj, "node")
-    full_proj = lax.all_gather(block_proj, "feat", axis=1, tiled=True)
+    full_proj = ring_gather(block_proj, "feat", 1)
     width = full_proj.shape[1] // lax.axis_size("node")
     columns = lax.dynamic_slice_in_dim(full_proj, lax.axis_index("node") * width, width, 1)
     term = lax.dot_general(

time: 142 us -> 132 us (0.930)
  waiting for transfers between devices: 107 us -> 91.4 us
  starting transfers between devices: 0.08 us -> 3.87 us
  local copies, waits for them, and re-layouts: 1.59 us -> 4.04 us
  matrix products: 20.1 us -> 18.5 us
    all_gather x1 -> x0, waiting for transfers between devices: 47.5 us -> none  [body(): full_proj = lax.all_gather(block_proj, 'feat', axis=1, tiled=True)]
    ppermute x0 -> x3, waiting for transfers between devices: none -> 32.9 us  [the longest x2 23.1 us: ring_gather(): from_left = lax.ppermute(from_left, axis, right)]
    ppermute x0 -> x3, starting transfers between devices: none -> 3.83 us  [the longest x1 2.34 us: ring_gather(): from_right = lax.ppermute(from_right, axis, left)]
    dynamic_update_slice x0 -> x4, local copies, waits for them, and re-layouts: none -> 2.26 us  [the longest x2 1.13 us: ring_gather(): lax.dynamic_update_slice_in_dim(out, from_left, (index - turn) % length *...]
    dot_general x1, matrix products: 6.61 us -> 5.07 us  [body(): lax.dot_general(block_proj, columns, (((0,), (0,)), ((), ())), precision=...]
  transfers between devices with their start and end apart: 3 -> 5, of which waited for: 3 -> 5; matrix products, arithmetic and copies ran while one was open for 0% -> 1% of each run, Pallas kernels for 0% -> 0%
where the time goes in v1:
time: 132 us; the launch traced here: 131 us
  waiting for transfers between devices  91.4 us (69%)
  matrix products  18.5 us (14%)
  between operations  13.4 us (10%)
  local copies, waits for them, and re-layouts  4.04 us (3%)
  starting transfers between devices  3.87 us (3%)
    psum x1, waiting for transfers between devices, body(): block_proj = lax.psum(partial_proj, 'node')  48.1 us
    ppermute x2, waiting for transfers between devices, ring_gather(): from_left = lax.ppermute(from_left, axis, right)  23.1 us
    dot_general x1, matrix products, body(): lax.dot_general(basis, local_data, (((0,), (0,)), ((), ())), precision=la...  13.5 us
    reduce_scatter x1, waiting for transfers between devices, body(): lax.psum_scatter(term * scale, 'tm', scatter_dimension=1, tiled=True)  10.3 us
    ppermute x1, waiting for transfers between devices, ring_gather(): from_right = lax.ppermute(from_right, axis, left)  9.73 us
    dot_general x1, matrix products, body(): lax.dot_general(block_proj, columns, (((0,), (0,)), ((), ())), precision=...  5.07 us
  transfers between devices with their start and end apart: 5, of which 5 were waited for; matrix products, arithmetic and copies ran while one was open for 1% of the time, Pallas kernels for 0%

profile of v1, /device:TPU:0, one launch (start us, length us, event | category | flops | bytes accessed | tf_op | source)
XLA Modules:
  0.0 131.3 jit_solution(3203274758813339894)
XLA Ops:
  6.5 0.0 copy-start
  6.5 0.0 all-reduce.2.cloned.1.call-start
  6.5 1.6 %copy-done = f32[4096,128]{1,0:T(8,128)S(1)} copy-done((f32[4096,128]{1,0:T(8,128)S(1)}, f32[4096,128]{1,0:T(8,128)}, u32[]{:S(2)}) %copy-start) | copy-done | bytes 2097176
  8.1 13.5 %fusion = f32[128,1024]{1,0:T(8,128)} fusion(f32[4096,128]{1,0:T(8,128)S(1)} %copy-done, f32[1,4096,1024]{2,1,0:T(8,128)} %param.2), kind=kOutput, calls=%fused_computation | convolution fusion | flops 6442450944 | bytes 19398656 | tf_op jit(solution)/shard_map/dot_general | solution.py:30
  21.6 0.0 all-reduce.2.cloned.1.call-update
  21.6 0.0 reduce-scatter.2.cloned.1.call-start
  21.7 48.1 %all-reduce.2.cloned.1.call-done = f32[128,1024]{1,0:T(8,128)} async-done(((f32[128,1024]{1,0:T(8,128)}), f32[128,1024]{1,0:T(8,128)}) %all-reduce.2.cloned.1.call-update) | async-done | bytes 524304 | tf_op jit(solution)/shard_map/psum | solution.py:38
  69.8 0.0 copy-start.1
  69.8 1.5 %collective-permute-start = (f32[128,1024]{1,0:T(8,128)}, f32[128,1024]{1,0:T(8,128)S(1)}, u32[]{:S(2)}, u32[]{:S(2)}) collective-permute-start(f32[128,1024]{1,0:T(8,128)} %all-reduce.2.cloned.1.call-done), channel_id=1, source_target_pairs={{0,2},{2,4},{4,6},{6,0},{1,3},{3,5},{5,7},{7,1},{8,10},{10,12},{12... | collective-permute-start | bytes 1572872 | tf_op jit(solution)/shard_map/ppermute | solution.py:16
  71.3 2.3 %collective-permute-start.1 = (f32[128,1024]{1,0:T(8,128)}, f32[128,1024]{1,0:T(8,128)}, u32[]{:S(2)}, u32[]{:S(2)}) collective-permute-start(f32[128,1024]{1,0:T(8,128)} %all-reduce.2.cloned.1.call-done), channel_id=1, source_target_pairs={{0,6},{2,0},{4,2},{6,4},{1,7},{3,1},{5,3},{7,5},{8,14},{10,8},{12,... | collective-permute-start | bytes 1572872 | tf_op jit(solution)/shard_map/ppermute | solution.py:21
  73.6 13.1 %collective-permute-done = f32[128,1024]{1,0:T(8,128)S(1)} collective-permute-done((f32[128,1024]{1,0:T(8,128)}, f32[128,1024]{1,0:T(8,128)S(1)}, u32[]{:S(2)}, u32[]{:S(2)}) %collective-permute-start) | collective-permute-done | bytes 524320 | tf_op jit(solution)/shard_map/ppermute | solution.py:16
  86.7 0.0 collective-permute-start.2
  86.7 0.2 broadcast_in_dim.3
  86.9 0.0 copy-done.1
  86.9 0.1 constant_dynamic-update-slice_fusion.3
  87.0 0.1 constant_dynamic-update-slice_fusion.2
  87.0 9.7 %collective-permute-done.1 = f32[128,1024]{1,0:T(8,128)} collective-permute-done((f32[128,1024]{1,0:T(8,128)}, f32[128,1024]{1,0:T(8,128)}, u32[]{:S(2)}, u32[]{:S(2)}) %collective-permute-start.1) | collective-permute-done | bytes 524320 | tf_op jit(solution)/shard_map/ppermute | solution.py:21
  96.8 1.1 constant_dynamic-update-slice_fusion.1
  97.9 10.1 %collective-permute-done.2 = f32[128,1024]{1,0:T(8,128)} collective-permute-done((f32[128,1024]{1,0:T(8,128)S(1)}, f32[128,1024]{1,0:T(8,128)}, u32[]{:S(2)}, u32[]{:S(2)}) %collective-permute-start.2) | collective-permute-done | bytes 524320 | tf_op jit(solution)/shard_map/ppermute | solution.py:16
  107.9 1.1 constant_dynamic-update-slice_fusion
  109.0 5.1 %convolution_multiply_fusion = f32[1024,1024]{1,0:T(8,128)} fusion(f32[128,1024]{1,0:T(8,128)S(1)} %copy-done.1, f32[128,4096]{1,0:T(8,128)S(1)} %constant_dynamic-update-slice_fusion, s32[]{:T(128)S(6)} %select_n.37), kind=kOutput, calls=%fused_computation.2 | convolution fusion | flops 1611661312 | bytes 5242884 | tf_op jit(solution)/shard_map/dot_general | solution.py:42
  114.1 0.0 reduce-scatter.2.cloned.1.call-update
  114.1 10.3 %reduce-scatter.2.cloned.1.call-done = f32[1024,512]{1,0:T(8,128)} async-done(((f32[1024,1024]{1,0:T(8,128)}), f32[1024,512]{1,0:T(8,128)}) %reduce-scatter.2.cloned.1.call-update) | async-done | bytes 2097168 | tf_op jit(solution)/shard_map/reduce_scatter | solution.py:49
Async XLA Ops:
  6.5 1.6 %copy-start = (f32[4096,128]{1,0:T(8,128)S(1)}, f32[4096,128]{1,0:T(8,128)}, u32[]{:S(2)}) copy-start(f32[4096,128]{1,0:T(8,128)} %param.3) | copy-start | bytes 6291460
  6.5 63.3 %all-reduce.2.cloned.1.call-start = ((), (), s32[]{:S(2)}) async-start(), calls=%async_computation.1 | async-start | bytes 1048576 | tf_op jit(solution)/shard_map/psum | solution.py:38
  21.6 102.8 %reduce-scatter.2.cloned.1.call-start = ((), (), s32[]{:S(2)}) async-start(), calls=%async_computation.2 | async-start | bytes 6291456 | tf_op jit(solution)/shard_map/reduce_scatter | solution.py:49
  69.8 17.1 %copy-start.1 = (f32[128,1024]{1,0:T(8,128)S(1)}, f32[128,1024]{1,0:T(8,128)}, u32[]{:S(2)}) copy-start(f32[128,1024]{1,0:T(8,128)} %all-reduce.2.cloned.1.call-done) | copy-start | bytes 1572868
  69.8 16.9 %collective-permute-start = (f32[128,1024]{1,0:T(8,128)}, f32[128,1024]{1,0:T(8,128)S(1)}, u32[]{:S(2)}, u32[]{:S(2)}) collective-permute-start(f32[128,1024]{1,0:T(8,128)} %all-reduce.2.cloned.1.call-done), channel_id=1, source_target_pairs={{0,2},{2,4},{4,6},{6,0},{1,3},{3,5},{5,7},{7,1},{8,10},{10,12},{12... | collective-permute-start | bytes 1572872 | tf_op jit(solution)/shard_map/ppermute | solution.py:16
  71.3 25.5 %collective-permute-start.1 = (f32[128,1024]{1,0:T(8,128)}, f32[128,1024]{1,0:T(8,128)}, u32[]{:S(2)}, u32[]{:S(2)}) collective-permute-start(f32[128,1024]{1,0:T(8,128)} %all-reduce.2.cloned.1.call-done), channel_id=1, source_target_pairs={{0,6},{2,0},{4,2},{6,4},{1,7},{3,1},{5,3},{7,5},{8,14},{10,8},{12,... | collective-permute-start | bytes 1572872 | tf_op jit(solution)/shard_map/ppermute | solution.py:21
  86.7 21.2 %collective-permute-start.2 = (f32[128,1024]{1,0:T(8,128)S(1)}, f32[128,1024]{1,0:T(8,128)}, u32[]{:S(2)}, u32[]{:S(2)}) collective-permute-start(f32[128,1024]{1,0:T(8,128)S(1)} %collective-permute-done), channel_id=1, source_target_pairs={{0,2},{2,4},{4,6},{6,0},{1,3},{3,5},{5,7},{7,1},{8,10},{10,12},{12... | collective-permute-start | bytes 1572872 | tf_op jit(solution)/shard_map/ppermute | solution.py:16
Sparse Core Ops, SparseCore 0:
  21.7 48.0 all-reduce.1
  114.2 10.1 reduce-scatter.1
